TPU v7x, 256 devices: a whole 4x4x8 slice. The times are simulated.
256 devices in a mesh: dp: 8 (over y, core), seq: 32 (over z, x).
Axes of the slice: x: 4, y: 4, z: 8, core: 2. Of those that a mesh axis runs over, the one named last changes fastest.
Arguments:
- queries: bfloat16 [8, 16384, 1024], P('dp', 'seq'), may hold values from -6 to 6
- keys: bfloat16 [8, 16384, 1024], P('dp', 'seq'), may hold values from -6 to 6
- values: bfloat16 [8, 16384, 1024], P('dp', 'seq'), may hold values from -6 to 6
- out_grad: bfloat16 [8, 16384, 2048], P('dp', 'seq'), may hold values from -6 to 6
- out_weight: bfloat16 [1024, 2048], P(('dp', 'seq')), may hold values from -0.125 to 0.125
- gain: float32 [1024], replicated, may hold values from 0.1 to 1.9
Outputs:
- query_grad: bfloat16 [8, 16384, 1024], P('dp', 'seq')
- key_grad: bfloat16 [8, 16384, 1024], P('dp', 'seq')
- value_grad: bfloat16 [8, 16384, 1024], P('dp', 'seq')
- weight_grad: float32 [1024, 2048], P(('dp', 'seq'))
- gain_grad: float32 [1024], replicated
All inputs are finite; a program needn't handle non-finite values.
Results may differ from a plain program's by a relative error of at most 0.015.
Values may be sent and summed in bfloat16 or wider, within the bound.
A program may use at most 128 MiB of HBM per device.

v0:
```python
import jax
import jax.numpy as jnp
from jax import lax
from jax.sharding import PartitionSpec as P

HEADS = 8
HEAD_DIM = 128
BLOCK = 512
HD = 1024


norm_eps = 1e-06


def prefix(x, axis, combine, identity, reverse):
    peers, here = (lax.axis_size(axis), lax.axis_index(axis))
    everything = lax.all_gather(x, axis)
    start = jnp.broadcast_to(jnp.asarray(identity, x.dtype), x.shape)

    def hop(k, before):
        at = peers - 1 - k if reverse else k
        reached = at > here if reverse else at < here
        new = combine(before, everything[at])
        return jnp.where(reached, new, before)

    return lax.fori_loop(0, peers, hop, start)


def causal_mask():
    places = jnp.arange(BLOCK, dtype=jnp.int32)
    return (places[None, :] <= places[:, None]).astype(jnp.float32)


def add_states(earlier, later):
    return earlier + later


def before_each(block_terms):
    running = jnp.cumsum(block_terms, axis=0)
    return jnp.concatenate([jnp.zeros_like(block_terms), running[:-1]], axis=0)


def after_each(block_terms):
    running = jnp.cumsum(block_terms[::-1], axis=0)[::-1]
    return jnp.concatenate([running[1:], jnp.zeros_like(block_terms)], axis=0)


def shards(queries, keys, values, out_grad, out_weight, gain):
    tok_count = queries.shape[1]
    blocks = tok_count // BLOCK
    block_shape = (blocks, BLOCK, HEADS, HEAD_DIM)
    query_blk = queries.reshape(block_shape)
    key_blk = keys.reshape(block_shape)
    value_blk = values.reshape(block_shape)
    grad_rows = out_grad[0]
    gain_heads = gain.reshape(HEADS, HEAD_DIM)
    causal = causal_mask()
    state_zero = jnp.zeros((HEADS, HEAD_DIM, HEAD_DIM), jnp.float32)
    block_kv = jnp.einsum("nshd,nshe->nhde", key_blk, value_blk, preferred_element_type=jnp.float32)
    within = before_each(block_kv)
    local_total = jnp.sum(block_kv, axis=0)
    before = prefix(local_total, "seq", add_states, state_zero, False)
    state_bf = (before[None] + within).astype(jnp.bfloat16)
    scores = jnp.einsum("nthd,nshd->nhts", query_blk, key_blk, preferred_element_type=jnp.float32)
    attn_bf = (scores * causal[None, None]).astype(jnp.bfloat16)
    outputs = jnp.einsum("nhts,nshd->nthd", attn_bf, value_blk, preferred_element_type=jnp.float32)
    outputs = outputs + jnp.einsum(
        "nthd,nhde->nthe", query_blk, state_bf, preferred_element_type=jnp.float32
    )
    rms = jnp.sqrt(jnp.mean(outputs * outputs, axis=-1, keepdims=True) + norm_eps)
    normed = outputs / rms
    unit_bf = (normed * gain_heads[None, None]).astype(jnp.bfloat16)
    unit_grad = lax.dot_general(
        grad_rows,
        lax.all_gather(out_weight, ("dp", "seq"), axis=0, tiled=True),
        (((1,), (1,)), ((), ())),
        preferred_element_type=jnp.float32,
    ).reshape(block_shape)
    gain_part = jnp.sum(unit_grad * normed, axis=(0, 1)).reshape(-1)
    scaled = unit_grad * gain_heads[None, None]
    middle = jnp.mean(scaled * normed, axis=-1, keepdims=True)
    attn_grad = ((scaled - normed * middle) / rms).astype(jnp.bfloat16)
    block_qg = jnp.einsum(
        "nthd,nthe->nhde", query_blk, attn_grad, preferred_element_type=jnp.float32
    )
    later_inside = after_each(block_qg)
    local_qg = jnp.sum(block_qg, axis=0)
    after = prefix(local_qg, "seq", add_states, state_zero, True)
    rev_bf = (after[None] + later_inside).astype(jnp.bfloat16)
    score_grad = (
        jnp.einsum("nthe,nshe->nhts", attn_grad, value_blk, preferred_element_type=jnp.float32)
        * causal[None, None]
    ).astype(jnp.bfloat16)
    query_g = jnp.einsum("nhts,nshd->nthd", score_grad, key_blk, preferred_element_type=jnp.float32)
    query_g = query_g + jnp.einsum(
        "nthe,nhde->nthd", attn_grad, state_bf, preferred_element_type=jnp.float32
    )
    key_g = jnp.einsum("nhts,nthd->nshd", score_grad, query_blk, preferred_element_type=jnp.float32)
    key_g = key_g + jnp.einsum(
        "nshe,nhde->nshd", value_blk, rev_bf, preferred_element_type=jnp.float32
    )
    value_g = jnp.einsum("nhts,nthe->nshe", attn_bf, attn_grad, preferred_element_type=jnp.float32)
    value_g = value_g + jnp.einsum(
        "nshd,nhde->nshe", key_blk, rev_bf, preferred_element_type=jnp.float32
    )
    unit_flat = unit_bf.reshape(tok_count, HD)
    data_count = lax.axis_size("dp")
    seq_count = lax.axis_size("seq")
    weight_sum = lax.psum_scatter(
        lax.dot_general(
            unit_flat, grad_rows, (((0,), (0,)), ((), ())), preferred_element_type=jnp.float32
        ),
        ("dp", "seq"),
        scatter_dimension=0,
        tiled=True,
    )
    gain_total = lax.psum(gain_part, ("dp", "seq"))
    factor = 1.0 / jnp.sqrt(jnp.float32(tok_count * data_count * seq_count))
    out_shape = (1, tok_count, HD)
    return (
        query_g.astype(jnp.bfloat16).reshape(out_shape),
        key_g.astype(jnp.bfloat16).reshape(out_shape),
        value_g.astype(jnp.bfloat16).reshape(out_shape),
        weight_sum * factor,
        gain_total * factor,
    )


def solution(mesh):
    placed = (
        P("dp", "seq", None),
        P("dp", "seq", None),
        P("dp", "seq", None),
        P("dp", "seq", None),
        P(("dp", "seq"), None),
        P(),
    )
    return jax.shard_map(
        shards,
        mesh=mesh,
        in_specs=placed,
        out_specs=(
            P("dp", "seq", None),
            P("dp", "seq", None),
            P("dp", "seq", None),
            P(("dp", "seq"), None),
            P(),
        ),
        check_vma=False,
    )
```

profile of v0, /device:TPU:2, one launch (start us, length us, event | category | flops | bytes accessed | tf_op | source)
XLA Modules:
  0.0 827.8 jit_solution(12613035057772357722)
XLA Ops:
  16.8 3.3 multiply_convert_fusion.1
  20.2 110.2 %all-gather.11.cloned.1.call-done = bf16[256,4,2048]{2,1,0:T(4,128)(2,1)} async-done(((bf16[1,4,2048]{2,1,0:T(4,128)(2,1)}), bf16[256,4,2048]{2,1,0:T(4,128)(2,1)}) %all-gather.11.cloned.1.call-update) | async-done | bytes 4194320 | tf_op jit(solution)/shard_map/all_gather | solution.py:75
  130.4 6.9 reshape.183
  137.3 5.9 fusion.5
  143.2 126.2 %all-gather.7.cloned.1.call-done = f32[256,128,128]{2,1,0:T(8,128)} async-done(((f32[8,128,128]{2,1,0:T(8,128)}), f32[256,128,128]{2,1,0:T(8,128)}) %all-gather.7.cloned.1.call-update) | async-done | bytes 16777232 | tf_op jit(solution)/shard_map/all_gather | solution.py:17
  269.5 65.3 %while.30 = (s32[]{:T(128)}, f32[8,128,128]{2,1,0:T(8,128)}, s32[]{:T(128)}, f32[32,8,128,128]{3,2,1,0:T(8,128)}, s32[]{:T(128)}, /*index=5*/s32[]{:T(128)}) while((s32[]{:T(128)}, f32[8,128,128]{2,1,0:T(8,128)}, s32[]{:T(128)}, f32[32,8,128,128]{3,2,1,0:T(8,128)}, s32[]{:T(128)}, /*index=5*/s32[]{:T(128)}) %tuple.92), condition=%wide.region_1.2_spmd.clone, body=%wide.region_0.0_spmd.clone.sunk | while | flops 393220 | bytes 1572957 | solution.py:26
  271.3 2.0 add_select_fusion.4
  279.5 2.0 add_select_fusion.4
  281.6 2.0 add_select_fusion.4
  283.6 2.0 add_select_fusion.4
  291.8 2.0 add_select_fusion.4
  293.8 2.0 add_select_fusion.4
  295.9 2.0 add_select_fusion.4
  304.1 2.0 add_select_fusion.4
  306.1 2.0 add_select_fusion.4
  308.1 2.0 add_select_fusion.4
  310.2 2.0 add_select_fusion.4
  318.4 2.0 add_select_fusion.4
  320.4 2.0 add_select_fusion.4
  336.7 3.8 fusion.2
  343.0 5.6 fusion.3
  351.4 2.1 copy.47
  356.4 2.5 fusion.1
  358.9 2.3 copy.52
  361.1 76.2 %psum.7 = f32[1024]{0:T(1024)S(1)} all-reduce(f32[1024]{0:T(1024)S(1)} %bitcast.111), channel_id=1, replica_groups=mesh['dp'=8,'seq'=32] {'dp','seq'}, use_global_device_ids=true, to_apply=%region_8.9 | all-reduce | flops 1024 | bytes 8192 | tf_op jit(solution)/shard_map/psum | solution.py:117
  438.0 4.3 fusion.7
  442.3 185.4 %all-reduce.3.cloned.1.call-done = f32[1024,2048]{1,0:T(8,128)} async-done(((f32[1024,2048]{1,0:T(8,128)}), f32[1024,2048]{1,0:T(8,128)}) %all-reduce.3.cloned.1.call-update) | async-done | bytes 8388624
  629.2 138.2 %all-gather.9.cloned.1.call-done = f32[256,128,128]{2,1,0:T(8,128)} async-done(((f32[8,128,128]{2,1,0:T(8,128)}), f32[256,128,128]{2,1,0:T(8,128)}) %all-gather.9.cloned.1.call-update) | async-done | bytes 16777232 | tf_op jit(solution)/shard_map/all_gather | solution.py:17
  767.4 40.2 %while.31 = (s32[]{:T(128)}, f32[8,128,128]{2,1,0:T(8,128)S(1)}, s32[]{:T(128)}, f32[32,8,128,128]{3,2,1,0:T(8,128)}, s32[]{:T(128)}, /*index=5*/s32[]{:T(128)}, s32[]{:T(128)}, s32[]{:T(128)}) while((s32[]{:T(128)}, f32[8,128,128]{2,1,0:T(8,128)S(1)}, s32[]{:T(128)}, f32[32,8,128,128]{3,2,1,0:T(8,128)}, s32[]{:T(128)}, ...), condition=%wide.region_5.6_spmd.clone, body=%wide.region_4.5_spmd.clone.sunk | while | flops 393224 | bytes 1573019 | solution.py:26
  811.8 2.4 copy.54
  814.2 4.8 fusion
  819.0 2.3 copy.53
  (113 shorter events, 103.7 us)
Async XLA Ops:
  7.2 130.2 %copy-start = (bf16[1,512,2048]{2,1,0:T(8,128)(2,1)S(1)}, bf16[1,512,2048]{2,1,0:T(8,128)(2,1)}, u32[]{:S(2)}) copy-start(bf16[1,512,2048]{2,1,0:T(8,128)(2,1)} %param.13) | copy-start | bytes 6291460
  7.2 123.2 %all-gather.11.cloned.1.call-start = ((), (), s32[]{:S(2)}) async-start(), calls=%async_computation.2 | async-start | bytes 4210688 | tf_op jit(solution)/shard_map/all_gather | solution.py:75
  7.9 261.5 %all-gather.7.cloned.1.call-start = ((), (), s32[]{:S(2)}) async-start(), calls=%async_computation | async-start | bytes 17301504 | tf_op jit(solution)/shard_map/all_gather | solution.py:17
  9.5 1.5 copy-start.7
  10.9 1.6 copy-start.12
  13.8 613.9 %all-reduce.3.cloned.1.call-start = ((), (), s32[]{:S(2)}) async-start(), calls=%async_computation.3 | async-start | bytes 16777216
  13.9 2.9 copy-start.8
  15.5 1.0 copy-start.4
  15.6 1.2 copy-start.10
  336.6 3.9 copy-start.15
  336.6 3.9 copy-start.16
  348.6 1.2 copy-start.3
  348.6 1.5 copy-start.5
  348.6 418.8 %all-gather.9.cloned.1.call-start = ((), (), s32[]{:S(2)}) async-start(), calls=%async_computation.1 | async-start | bytes 17301504 | tf_op jit(solution)/shard_map/all_gather | solution.py:17
  353.4 1.6 copy-start.11
  355.0 1.4 copy-start.13
  356.4 2.5 copy-start.2
  807.6 1.8 copy-start.9
  807.6 2.7 copy-start.14
  811.8 2.4 copy-start.6
  814.2 7.0 copy-start.1
Sparse Core Ops, SparseCore 0:
  11.7 118.6 all-gather.10
  133.5 135.8 all-gather.6
  348.7 278.9 all-reduce.2
  630.2 137.2 all-gather.8
where the time goes:
time: 832 us; the launch traced here: 828 us
  waiting for transfers between devices  561 us (67%)
  other arithmetic  109 us (13%)
  blocking collectives  76.2 us (9%)
  matrix products  40.8 us (5%)
  local copies, waits for them, and re-layouts  25.4 us (3%)
  between operations  14 us (2%)
    all_gather x2, waiting for transfers between devices, prefix(): everything = lax.all_gather(x, axis)  264 us
    unnamed x5, waiting for transfers between devices  186 us
    all_gather x1, waiting for transfers between devices, shards(): lax.all_gather(out_weight, ('dp', 'seq'), axis=0, tiled=True)  110 us
    select_n x64, other arithmetic, hop(): return jnp.where(reached, new, before)  105 us
    psum x1, blocking collectives, shards(): gain_total = lax.psum(gain_part, ('dp', 'seq'))  76.2 us
    unnamed x41, local copies, waits for them, and re-layouts  21.9 us
  transfers between devices with their start and end apart: 4, of which 4 were waited for; matrix products, arithmetic and copies ran while one was open for 5% of the time, Pallas kernels for 0%

commit v1 on v0

v1 whole, which is shorter than its diff:
```python
import functools

import jax
import jax.numpy as jnp
from jax import lax
from jax.experimental import pallas as pl
from jax.experimental.pallas import tpu as pltpu
from jax.sharding import PartitionSpec as P

HEADS = 8
HEAD_DIM = 128
NORM_EPS = 1e-06
XDIM = 4
YDIM = 4
CORES = 2
MESH = pl.DeviceIdType.MESH
F32 = jnp.float32
BF16 = jnp.bfloat16

NT = (((1,), (1,)), ((), ()))
TN = (((0,), (0,)), ((), ()))


def mm(a, b, dims=(((1,), (0,)), ((), ()))):
    return lax.dot_general(a, b, dims, preferred_element_type=F32)


def kernel(nz, factor, q_hbm, k_hbm, v_hbm, g_hbm, w_hbm, gain_ref,
           qo_hbm, ko_hbm, vo_hbm, wo_ref, go_ref,
           q, k, v, g, oq, ok, ov, wx, asm, wbuf, attn, outp, unit, ag, kpart, vpart,
           kvs, ra, tz, po, st, qgs, rra, rtz, rpo, rst,
           wgp, prt, ys2, yr2, ysf, yrc, ysb, yrs, fsum, wself,
           zus, zur, zds, zdr, xs, xr, gx, gz, gy, gc,
           in_s, out_s, wx_s, wx_r, wz_s, wz_r, wy_s, wy_r, wp_s, wp_r,
           sx_s, sx_r, sz_s, sz_r, sb_s, sb_r, rp_s, rp_r, ry_s, ry_r, rz_s, rz_r, rx_s, rx_r,
           gx_s, gx_r, gz_s, gz_r, gy_s, gy_r, gc_s, gc_r):
    nx = XDIM
    hx = HEADS // nx
    half = nz // 2
    me_dp = lax.axis_index("dp")
    me_seq = lax.axis_index("seq")
    y = me_dp // CORES
    c = me_dp % CORES
    z = me_seq // nx
    x = me_seq % nx
    step = 1 - 2 * c
    yf = (y + step + YDIM) % YDIM
    yb = (y - step + YDIM) % YDIM
    y2 = (y + 2) % YDIM
    zup = (z + 1) % nz
    zdn = (z + nz - 1) % nz
    tokens = q.shape[0]
    hd = HEAD_DIM
    rows = wx.shape[1]

    to_f = (yf * CORES + c, me_seq)
    to_b = (yb * CORES + c, me_seq)
    to_p = (y * CORES + 1 - c, me_seq)
    to_up = (me_dp, zup * nx + x)
    to_dn = (me_dp, zdn * nx + x)

    def to_x(j):
        return (me_dp, z * nx + j)

    pending = []

    def send(src, dst, ss, rs, dev):
        copy = pltpu.make_async_remote_copy(
            src_ref=src, dst_ref=dst, send_sem=ss, recv_sem=rs, device_id=dev, device_id_type=MESH)
        copy.start()
        pending.append(copy)

    def arrived(dst, ss, rs, dev):
        pltpu.make_async_remote_copy(
            src_ref=dst, dst_ref=dst, send_sem=ss, recv_sem=rs, device_id=dev, device_id_type=MESH).wait_recv()

    def cols(h):
        return pl.ds(pl.multiple_of(h * hd, hd), hd)

    barrier = pltpu.get_barrier_semaphore()
    peers = [to_x((x + i) % nx) for i in range(1, nx)] + [to_up, to_dn, to_f, to_b, to_p]
    for peer in peers:
        pl.semaphore_signal(barrier, inc=1, device_id=peer, device_id_type=MESH)

    loads = [pltpu.make_async_copy(a, b, in_s.at[i]) for i, (a, b) in enumerate(
        [(k_hbm.at[0], k), (v_hbm.at[0], v), (w_hbm, wx.at[x]), (q_hbm.at[0], q), (g_hbm.at[0], g)])]
    for load in loads:
        load.start()
    pl.semaphore_wait(barrier, len(peers))

    for i in range(1, nx):
        send(w_hbm, wx.at[x], wx_s.at[i], wx_r.at[x], to_x((x + i) % nx))

    loads[0].wait()
    loads[1].wait()

    def kv_head(h, _):
        kvs[h // hx, h % hx] = mm(k[:, cols(h)], v[:, cols(h)], TN).astype(BF16)
        return 0

    lax.fori_loop(0, HEADS, kv_head, 0)

    def scan_x_send(n, snd, recv):
        for i in range(1, nx):
            j = (x + i) % nx
            send(snd.at[j], recv.at[x], sx_s.at[n, i], sx_r.at[n, x], to_x(j))
        recv[x] = snd[x]

    def scan_x_sum(n, recv, ring):
        for i in range(1, nx):
            j = (x + i) % nx
            arrived(recv.at[j], sx_s.at[n, i], sx_r.at[n, j], to_x(j))
        total = recv[0].astype(F32)
        for j in range(1, nx):
            total = total + recv[j].astype(F32)
        ring[z] = total.astype(BF16)

    def ring_start(buf, blk, ss, rs):
        send(buf.at[blk(z)], buf.at[blk(z)], ss.at[0, 0], rs.at[z], to_up)
        if half > 1:
            send(buf.at[blk(z)], buf.at[blk(z)], ss.at[1, 0], rs.at[z], to_dn)

    def ring_step(buf, blk, ss, rs, n):
        up = (z + nz - n) % nz
        arrived(buf.at[blk(up)], ss.at[0, n], rs.at[up], to_up)
        if n < half:
            send(buf.at[blk(up)], buf.at[blk(up)], ss.at[0, n], rs.at[up], to_up)
            dn = (z + n) % nz
            arrived(buf.at[blk(dn)], ss.at[1, n], rs.at[dn], to_dn)
            if n < half - 1:
                send(buf.at[blk(dn)], buf.at[blk(dn)], ss.at[1, n], rs.at[dn], to_dn)

    def scan_finish(n, recv, ring, out, state, reverse):
        acc = jnp.zeros((hx, hd, hd), F32)
        for zz in range(nz):
            keep = (z < zz) if reverse else (zz < z)
            acc = acc + ring[zz].astype(F32) * keep.astype(F32)
        for j in (range(nx - 1, -1, -1) if reverse else range(nx)):
            out[j] = acc.astype(BF16)
            acc = acc + recv[j].astype(F32)
        for i in range(1, nx):
            j = (x + i) % nx
            send(out.at[j], state.at[x], sb_s.at[n, i], sb_r.at[n, x], to_x(j))
        state[x] = out[x]

    def scan_wait(n, state):
        for i in range(1, nx):
            j = (x + i) % nx
            arrived(state.at[j], sb_s.at[n, i], sb_r.at[n, j], to_x(j))

    scan_x_send(0, kvs, ra)

    for i in range(1, nx):
        j = (x + i) % nx
        arrived(wx.at[j], wx_s.at[i], wx_r.at[j], to_x(j))
    loads[2].wait()
    for j in range(nx):
        asm[j * rows:(j + 1) * rows, :] = wx[j].astype(F32)

    def wblk(zz):
        return me_dp * nz + zz

    wbuf[wblk(z)] = asm[...].astype(BF16)

    def w_column(zz):
        blk = wbuf.at[wblk(zz)]
        send(blk, blk, wy_s.at[0, zz], wy_r.at[0, zz], to_f)
        send(blk, blk, wy_s.at[1, zz], wy_r.at[1, zz], to_b)

    def w_forward(zz):
        blk = wbuf.at[(yb * CORES + c) * nz + zz]
        arrived(blk, wy_s.at[2, zz], wy_r.at[0, zz], to_f)
        send(blk, blk, wy_s.at[2, zz], wy_r.at[2, zz], to_f)

    def w_group(yy, cc):
        return wbuf.at[pl.ds((yy * CORES + cc) * nz, nz)]

    scan_x_sum(0, ra, tz)
    ring_start(wbuf, wblk, wz_s, wz_r)
    w_column(z)
    ident = lambda zz: zz
    ring_start(tz, ident, sz_s.at[0], sz_r.at[0])

    loads[3].wait()
    causal = (lax.broadcasted_iota(jnp.int32, (tokens, tokens), 0)
              >= lax.broadcasted_iota(jnp.int32, (tokens, tokens), 1))

    def attn_head(h, _):
        a = jnp.where(causal, mm(q[:, cols(h)], k[:, cols(h)], NT), 0.0).astype(BF16)
        attn[h] = a
        outp[:, cols(h)] = mm(a, v[:, cols(h)])
        return 0

    per = HEADS // half
    for n in range(1, half + 1):
        ring_step(tz, ident, sz_s.at[0], sz_r.at[0], n)
        ring_step(wbuf, wblk, wz_s, wz_r, n)
        w_column((z + nz - n) % nz)
        if n < half:
            w_column((z + n) % nz)
        w_forward((z + nz - n + 1) % nz)
        if n > 1:
            w_forward((z + n - 1) % nz)
        if n == half:
            scan_finish(0, ra, tz, po, st, False)
        lax.fori_loop((n - 1) * per, n * per, attn_head, 0)
    send(w_group(y, c), w_group(y, c), wp_s.at[y], wp_r.at[y], to_p)
    w_forward((z + nz - half) % nz)
    send(w_group(yb, c), w_group(yb, c), wp_s.at[yb], wp_r.at[yb], to_p)
    order = [z]
    for n in range(1, half + 1):
        order.append((z + nz - n) % nz)
        if n < half:
            order.append((z + n) % nz)
    for zz in order:
        arrived(wbuf.at[(yf * CORES + c) * nz + zz], wy_s.at[1, zz], wy_r.at[1, zz], to_b)
    send(w_group(yf, c), w_group(yf, c), wp_s.at[yf], wp_r.at[yf], to_p)
    for zz in order:
        arrived(wbuf.at[(y2 * CORES + c) * nz + zz], wy_s.at[2, zz], wy_r.at[2, zz], to_f)
    send(w_group(y2, c), w_group(y2, c), wp_s.at[y2], wp_r.at[y2], to_p)
    loads[4].wait()
    scan_wait(0, st)
    for yy in (y, yb, yf, y2):
        grp = w_group(yy, 1 - c)
        arrived(grp, wp_s.at[yy], wp_r.at[yy], to_p)

    def norm_pair(p, _):
        w2 = wbuf[pl.ds(p * 2 * nz, 2 * nz)].reshape(2 * hd, wbuf.shape[-1])
        ug2 = mm(g[...], w2, NT)
        for i in range(2):
            h = p * 2 + i
            ug = ug2[:, i * hd:(i + 1) * hd]
            qh = q[:, cols(h)]
            o = outp[:, cols(h)] + mm(qh, st[h // hx, h % hx])
            inv = 1.0 / jnp.sqrt(jnp.mean(o * o, axis=-1, keepdims=True) + NORM_EPS)
            normed = o * inv
            gain = gain_ref[pl.ds(h, 1), :]
            unit[:, cols(h)] = (normed * gain).astype(BF16)
            gx[x, pl.ds(h, 1), :] = jnp.sum(ug * normed, axis=0, keepdims=True)
            scaled = ug * gain
            m = jnp.mean(scaled * normed, axis=-1, keepdims=True)
            a = ((scaled - normed * m) * inv).astype(BF16)
            ag[:, cols(h)] = a
            qgs[h // hx, h % hx] = mm(qh, a, TN).astype(BF16)
        return 0

    lax.fori_loop(0, HEADS // 2, norm_pair, 0)

    scan_x_send(1, qgs, rra)
    for i in range(1, nx):
        send(gx.at[x], gx.at[x], gx_s.at[i], gx_r.at[x], to_x((x + i) % nx))

    def wgrad(yy, cc):
        h = yy * CORES + cc
        return mm(unit[:, cols(h)], g[...], TN).reshape(nz, hd // nz, g.shape[-1])

    for yy in (y2, yb, yf, y):
        wgp[yy] = wgrad(yy, 1 - c).astype(BF16)
        send(wgp.at[yy], prt.at[yy], rp_s.at[yy], rp_r.at[yy], to_p)

    def chip_sum(yy):
        own = wgrad(yy, c)
        arrived(prt.at[yy], rp_s.at[yy], rp_r.at[yy], to_p)
        return own + prt[yy].astype(F32)

    zorder = []
    for n in range(half):
        zorder.append((z + half - n) % nz)
        if n < half - 1:
            zorder.append((z + nz - half + 1 + n) % nz)
    zorder.append(z)

    ys2[...] = chip_sum(y2).astype(BF16)
    for zz in zorder:
        send(ys2.at[zz], yr2.at[zz], ry_s.at[0, zz], ry_r.at[0, zz], to_f)
    ysb[...] = chip_sum(yb).astype(BF16)
    for zz in zorder:
        send(ysb.at[zz], yrs.at[zz], ry_s.at[1, zz], ry_r.at[1, zz], to_b)

    scan_x_sum(1, rra, rtz)
    ring_start(rtz, ident, sz_s.at[1], sz_r.at[1])
    for i in range(1, nx):
        j = (x + i) % nx
        arrived(gx.at[j], gx_s.at[i], gx_r.at[j], to_x(j))
    gz[z] = jnp.sum(gx[...], axis=0)
    ring_start(gz, ident, gz_s, gz_r)

    fsum[...] = chip_sum(yf)
    wself[...] = chip_sum(y)

    def y_forward(zz):
        arrived(yr2.at[zz], ry_s.at[0, zz], ry_r.at[0, zz], to_f)
        ysf[zz] = (fsum[zz] + yr2[zz].astype(F32)).astype(BF16)
        send(ysf.at[zz], yrc.at[zz], ry_s.at[2, zz], ry_r.at[2, zz], to_f)

    def grad_head(h, _):
        qh, kh, vh, ah = q[:, cols(h)], k[:, cols(h)], v[:, cols(h)], ag[:, cols(h)]
        sg = jnp.where(causal, mm(ah, vh, NT), 0.0).astype(BF16)
        oq[:, cols(h)] = (mm(sg, kh) + mm(ah, st[h // hx, h % hx], NT)).astype(BF16)
        kpart[:, cols(h)] = mm(sg, qh, TN)
        vpart[:, cols(h)] = mm(attn[h], ah, TN)
        return 0

    for n in range(1, half + 1):
        y_forward(zorder[2 * n - 2])
        y_forward(zorder[2 * n - 1])
        ring_step(rtz, ident, sz_s.at[1], sz_r.at[1], n)
        ring_step(gz, ident, gz_s, gz_r, n)
        if n == half:
            scan_finish(1, rra, rtz, rpo, rst, True)
        lax.fori_loop((n - 1) * per, n * per, grad_head, 0)

    stores = [pltpu.make_async_copy(oq, qo_hbm.at[0], out_s.at[0])]
    stores[0].start()
    gy[y] = jnp.sum(gz[...], axis=0)
    send(gy.at[y], gy.at[y], gy_s.at[0], gy_r.at[0], to_f)
    send(gy.at[y], gy.at[y], gy_s.at[1], gy_r.at[1], to_b)

    def block(zz):
        arrived(yrc.at[zz], ry_s.at[2, zz], ry_r.at[2, zz], to_f)
        arrived(yrs.at[zz], ry_s.at[1, zz], ry_r.at[1, zz], to_b)
        return wself[zz] + yrc[zz].astype(F32) + yrs[zz].astype(F32)

    def z_step(n):
        val = block((z + half - n) % nz)
        if n > 0:
            arrived(zur.at[n - 1], rz_s.at[0, n - 1], rz_r.at[0, n - 1], to_up)
            val = val + zur[n - 1].astype(F32)
        zus[n] = val.astype(BF16)
        send(zus.at[n], zur.at[n], rz_s.at[0, n], rz_r.at[0, n], to_up)
        if n < half - 1:
            val = block((z + nz - half + 1 + n) % nz)
            if n > 0:
                arrived(zdr.at[n - 1], rz_s.at[1, n - 1], rz_r.at[1, n - 1], to_dn)
                val = val + zdr[n - 1].astype(F32)
            zds[n] = val.astype(BF16)
            send(zds.at[n], zdr.at[n], rz_s.at[1, n], rz_r.at[1, n], to_dn)

    z_step(0)
    arrived(gy.at[yb], gy_s.at[0], gy_r.at[0], to_f)
    send(gy.at[yb], gy.at[yb], gy_s.at[2], gy_r.at[2], to_f)

    scan_wait(1, rst)

    def last_head(h, _):
        rev = rst[h // hx, h % hx]
        ok[:, cols(h)] = (kpart[:, cols(h)] + mm(v[:, cols(h)], rev, NT)).astype(BF16)
        ov[:, cols(h)] = (vpart[:, cols(h)] + mm(k[:, cols(h)], rev)).astype(BF16)
        return 0

    lax.fori_loop(0, HEADS, last_head, 0)
    for i, (a, b) in enumerate([(ok, ko_hbm), (ov, vo_hbm)]):
        stores.append(pltpu.make_async_copy(a, b.at[0], out_s.at[i + 1]))
        stores[-1].start()

    for n in range(1, half):
        z_step(n)
    arrived(gy.at[yf], gy_s.at[1], gy_r.at[1], to_b)
    arrived(gy.at[y2], gy_s.at[2], gy_r.at[2], to_f)
    gc[c] = jnp.sum(gy[...], axis=0)
    send(gc.at[c], gc.at[c], gc_s.at[0], gc_r.at[0], to_p)

    fin = block(z)
    arrived(zur.at[half - 1], rz_s.at[0, half - 1], rz_r.at[0, half - 1], to_up)
    fin = fin + zur[half - 1].astype(F32)
    if half > 1:
        arrived(zdr.at[half - 2], rz_s.at[1, half - 2], rz_r.at[1, half - 2], to_dn)
        fin = fin + zdr[half - 2].astype(F32)
    for j in range(nx):
        xs[j] = fin[j * rows:(j + 1) * rows, :]
    for i in range(1, nx):
        j = (x + i) % nx
        send(xs.at[j], xr.at[x], rx_s.at[i], rx_r.at[x], to_x(j))
    xr[x] = xs[x]
    arrived(gc.at[1 - c], gc_s.at[0], gc_r.at[0], to_p)
    go_ref[...] = (gc[0] + gc[1]) * factor
    for i in range(1, nx):
        j = (x + i) % nx
        arrived(xr.at[j], rx_s.at[i], rx_r.at[j], to_x(j))
    wo_ref[...] = jnp.sum(xr[...], axis=0) * factor

    for copy in pending:
        copy.wait_send()
    for store in stores:
        store.wait()


def shards(interpret, queries, keys, values, out_grad, out_weight, gain):
    nx = XDIM
    ndp = lax.axis_size("dp")
    nseq = lax.axis_size("seq")
    nz = nseq // nx
    hx = HEADS // nx
    half = nz // 2
    hd = HEAD_DIM
    tok = queries.shape[1]
    d = out_grad.shape[2]
    width = HEADS * hd
    rows = out_weight.shape[0]
    br = rows * nx
    total = tok * ndp * nseq
    factor = 1.0 / float(total) ** 0.5
    vm = pltpu.VMEM
    dma = pltpu.SemaphoreType.DMA
    blocks = vm((nz, br, d), BF16)
    states = vm((nx, hx, hd, hd), BF16)
    ring = vm((nz, hx, hd, hd), BF16)
    flat = vm((tok, width), BF16)
    flat32 = vm((tok, width), F32)
    dn = max(half - 1, 1)
    scratch = [
        flat, flat, flat, vm((tok, d), BF16), flat, flat, flat,
        vm((nx, rows, d), BF16), vm((br, d), F32), vm((ndp * nz, br, d), BF16),
        vm((HEADS, tok, tok), BF16), flat32, flat, flat, flat32, flat32,
        states, states, ring, states, states, states, states, ring, states, states,
        vm((YDIM, nz, br, d), BF16), vm((YDIM, nz, br, d), BF16),
        blocks, blocks, blocks, blocks, blocks, blocks, vm((nz, br, d), F32), vm((nz, br, d), F32),
        vm((half, br, d), BF16), vm((half, br, d), BF16), vm((dn, br, d), BF16), vm((dn, br, d), BF16),
        vm((nx, rows, d), F32), vm((nx, rows, d), F32),
        vm((nx, HEADS, hd), F32), vm((nz, HEADS, hd), F32), vm((YDIM, HEADS, hd), F32), vm((CORES, HEADS, hd), F32),
        dma((5,)), dma((3,)), dma((nx,)), dma((nx,)), dma((2, half + 1)), dma((nz,)),
        dma((3, nz)), dma((3, nz)), dma((YDIM,)), dma((YDIM,)),
        dma((2, nx)), dma((2, nx)), dma((2, 2, half + 1)), dma((2, nz)), dma((2, nx)), dma((2, nx)),
        dma((YDIM,)), dma((YDIM,)), dma((3, nz)), dma((3, nz)), dma((2, half)), dma((2, half)),
        dma((nx,)), dma((nx,)),
        dma((nx,)), dma((nx,)), dma((2, half + 1)), dma((nz,)), dma((3,)), dma((3,)), dma((1,)), dma((1,)),
    ]
    any_spec = pl.BlockSpec(memory_space=pl.ANY)
    vspec = pl.BlockSpec(memory_space=pltpu.VMEM)
    grad = jax.ShapeDtypeStruct((1, tok, width), BF16)
    flops = 2 * tok * width * (2 * d + 6 * tok + 7 * hd)
    qg, kg, vg, wg, gg = pl.pallas_call(
        functools.partial(kernel, nz, factor),
        out_shape=(grad, grad, grad,
                   jax.ShapeDtypeStruct((rows, d), F32), jax.ShapeDtypeStruct((HEADS, hd), F32)),
        in_specs=[any_spec] * 5 + [vspec],
        out_specs=(any_spec, any_spec, any_spec, vspec, vspec),
        scratch_shapes=scratch,
        compiler_params=pltpu.CompilerParams(
            collective_id=0, has_side_effects=True, vmem_limit_bytes=62 * 1024 * 1024),
        cost_estimate=pl.CostEstimate(flops=flops, bytes_accessed=16 * 1024 * 1024, transcendentals=0),
        interpret=interpret,
    )(queries, keys, values, out_grad, out_weight, gain.reshape(HEADS, hd))
    return qg, kg, vg, wg, gg.reshape(width)


def solution(mesh, interpret=False):
    tokens = P("dp", "seq", None)
    placed = (tokens, tokens, tokens, tokens, P(("dp", "seq"), None), P())
    return jax.shard_map(
        functools.partial(shards, interpret),
        mesh=mesh,
        in_specs=placed,
        out_specs=(tokens, tokens, tokens, P(("dp", "seq"), None), P()),
        check_vma=False,
    )
```

time: 832 us -> 97.4 us (0.12)
  waiting for transfers between devices: 561 us -> 0 us
  other arithmetic: 109 us -> 0 us
  Pallas kernels: 0 us -> 90.5 us
  blocking collectives: 76.2 us -> 0 us
  matrix products: 40.8 us -> 0 us
  local copies, waits for them, and re-layouts: 25.4 us -> 5.57 us
  between operations: 14 us -> 0.66 us
    all_gather x3 -> x0, waiting for transfers between devices: 375 us -> none  [the longest x2 264 us: prefix(): everything = lax.all_gather(x, axis)]
    unnamed x5 -> x0, waiting for transfers between devices: 186 us -> none
    select_n x64 -> x0, other arithmetic: 105 us -> none  [hop(): return jnp.where(reached, new, before)]
    pallas_call x0 -> x1, Pallas kernels: none -> 90.5 us  [shards(): pl.pallas_call(functools.partial(kernel, nz, factor), out_shape=(grad, gr...]
    psum x1 -> x0, blocking collectives: 76.2 us -> none  [shards(): gain_total = lax.psum(gain_part, ('dp', 'seq'))]
    dot_general x13 -> x0, matrix products: 34.9 us -> none  [the longest x1 5.58 us: shards(): lax.dot_general(unit_flat, grad_rows, (((0,), (0,)), ((), ())), preferred...]
    unnamed x41 -> x13, local copies, waits for them, and re-layouts: 21.9 us -> 5.57 us
  transfers between devices with their start and end apart: 4 -> 0, of which waited for: 4 -> 0; matrix products, arithmetic and copies ran while one was open for 5% -> 0% of each run, Pallas kernels for 0% -> 0%
where the time goes in v1:
time: 97.4 us; the launch traced here: 96.7 us
  Pallas kernels  90.5 us (93%)
  local copies, waits for them, and re-layouts  5.57 us (6%)
    pallas_call x1, Pallas kernels, shards(): pl.pallas_call(functools.partial(kernel, nz, factor), out_shape=(grad, gr...  90.5 us
    unnamed x13, local copies, waits for them, and re-layouts  5.57 us

profile of v1, /device:TPU:2, one launch (start us, length us, event | category | flops | bytes accessed | tf_op | source)
XLA Modules:
  0.0 96.7 jit_solution(11796313597331276388)
XLA Ops:
  0.6 90.5 %shard_map.101 = (bf16[1,512,1024]{2,1,0:T(8,128)(2,1)}, bf16[1,512,1024]{2,1,0:T(8,128)(2,1)}, bf16[1,512,1024]{2,1,0:T(8,128)(2,1)}, f32[4,2048]{1,0:T(4,128)}, f32[8,128]{1,0:T(8,128)}) custom-call(bf16[1,512,1024]{2,1,0:T(8,128)(2,1)} %q_hbm.1, bf16[1,512,1024]{2,1,0:T(8,128)(2,1)} %k_hbm.1, bf16[1,512,1024]{2,1,0:T(8,128)(2,1)} %v_hbm.1, ...), custom_call_target="tpu_custom_call" | custom-call | flops 8455716864 | bytes 16777216 | tf_op jit(solution)/shard_map/pallas_call | solution.py:432
  91.1 0.0 copy-start.1
  91.1 0.0 copy-start
  91.1 2.4 %copy.16 = bf16[1,512,1024]{2,1,0:T(8,128)(2,1)} copy(bf16[1,512,1024]{2,1,0:T(8,128)(2,1)} %get-tuple-element.20) | data formatting | bytes 2097152
  93.5 0.0 copy-done.1
  93.5 0.0 copy-start.2
  93.5 0.0 copy-start.3
  93.5 1.0 %copy.17 = bf16[1,512,1024]{2,1,0:T(8,128)(2,1)} copy(bf16[1,512,1024]{2,1,0:T(8,128)(2,1)S(1)} %copy-done.1) | data formatting | bytes 2097152
  94.5 0.0 copy-done
  94.5 1.0 %copy.18 = bf16[1,512,1024]{2,1,0:T(8,128)(2,1)} copy(bf16[1,512,1024]{2,1,0:T(8,128)(2,1)S(1)} %copy-done) | data formatting | bytes 2097152
  95.5 0.0 copy-done.2
  95.5 0.6 copy.19
  96.1 0.0 copy-done.3
  96.1 0.6 copy.20
Async XLA Ops:
  91.1 2.4 %copy-start.1 = (bf16[1,512,1024]{2,1,0:T(8,128)(2,1)S(1)}, bf16[1,512,1024]{2,1,0:T(8,128)(2,1)}, u32[]{:S(2)}) copy-start(bf16[1,512,1024]{2,1,0:T(8,128)(2,1)} %get-tuple-element.21) | copy-start | bytes 3145732
  91.1 3.4 %copy-start = (bf16[1,512,1024]{2,1,0:T(8,128)(2,1)S(1)}, bf16[1,512,1024]{2,1,0:T(8,128)(2,1)}, u32[]{:S(2)}) copy-start(bf16[1,512,1024]{2,1,0:T(8,128)(2,1)} %get-tuple-element.22) | copy-start | bytes 3145732
  93.5 1.9 %copy-start.2 = (f32[4,2048]{1,0:T(4,128)S(1)}, f32[4,2048]{1,0:T(4,128)}, u32[]{:S(2)}) copy-start(f32[4,2048]{1,0:T(4,128)} %get-tuple-element.23) | copy-start | bytes 98308
  93.5 2.6 %copy-start.3 = (f32[8,128]{1,0:T(8,128)S(1)}, f32[8,128]{1,0:T(8,128)}, u32[]{:S(2)}) copy-start(f32[8,128]{1,0:T(8,128)} %get-tuple-element.14) | copy-start | bytes 12292

commit v2 on v1

v2 whole, which is shorter than its diff:
```python
import functools

import jax
import jax.numpy as jnp
from jax import lax
from jax.experimental import pallas as pl
from jax.experimental.pallas import tpu as pltpu
from jax.sharding import PartitionSpec as P

HEADS = 8
HEAD_DIM = 128
NORM_EPS = 1e-06
XDIM = 4
YDIM = 4
CORES = 2
MESH = pl.DeviceIdType.MESH
F32 = jnp.float32
BF16 = jnp.bfloat16

NT = (((1,), (1,)), ((), ()))
TN = (((0,), (0,)), ((), ()))


def mm(a, b, dims=(((1,), (0,)), ((), ()))):
    return lax.dot_general(a, b, dims, preferred_element_type=F32)


def kernel(nz, factor, q_hbm, k_hbm, v_hbm, g_hbm, w_hbm, gain_ref,
           qo_hbm, ko_hbm, vo_hbm, wo_ref, go_ref,
           q, k, v, g, oq, ok, ov, wx, asm, wbuf, attn, outp, inv_ref, unit, ag, kpart, vpart,
           kvs, ra, ts, tr, es, er, po, st, qgs, rra, rts, rtr, res, rer, rpo, rst,
           wgp, prt, ys2, yr2, ysf, yrc, ysb, yrs, fsum, wself, zs, zr, xs, xr, gx, gz, gy, gc,
           in_s, out_s, wx_s, wx_r, wz_s, wz_r, wy_s, wy_r, wp_s, wp_r,
           sx_s, sx_r, sz_s, sz_r, sb_s, sb_r, rp_s, rp_r, ry_s, ry_r, rz_s, rz_r, rx_s, rx_r,
           gx_s, gx_r, gz_s, gz_r, gy_s, gy_r, gc_s, gc_r):
    nx = XDIM
    hx = HEADS // nx
    me_dp = lax.axis_index("dp")
    me_seq = lax.axis_index("seq")
    y = me_dp // CORES
    c = me_dp % CORES
    z = me_seq // nx
    x = me_seq % nx
    step = 1 - 2 * c
    yf = (y + step + YDIM) % YDIM
    yb = (y - step + YDIM) % YDIM
    y2 = (y + 2) % YDIM
    tokens = q.shape[0]
    hd = HEAD_DIM
    rows = wx.shape[1]

    def to_x(j):
        return (me_dp, z * nx + j)

    def to_y(j):
        return (j * CORES + c, me_seq)

    def to_z(j):
        return (me_dp, j * nx + x)

    to_f = to_y(yf)
    to_b = to_y(yb)
    to_p = (y * CORES + 1 - c, me_seq)

    xs_other = [(x + i) % nx for i in ((2, 1, 3) if nx == 4 else range(1, nx))]
    z_offsets = sorted(range(1, nz), key=lambda o: -min(o, nz - o))
    zs_other = [(z + o) % nz for o in z_offsets]

    pending = []

    def send(src, dst, ss, rs, dev):
        copy = pltpu.make_async_remote_copy(
            src_ref=src, dst_ref=dst, send_sem=ss, recv_sem=rs, device_id=dev, device_id_type=MESH)
        copy.start()
        pending.append(copy)

    def arrived(dst, ss, rs, dev):
        pltpu.make_async_remote_copy(
            src_ref=dst, dst_ref=dst, send_sem=ss, recv_sem=rs, device_id=dev, device_id_type=MESH).wait_recv()

    def cols(h):
        return pl.ds(pl.multiple_of(h * hd, hd), hd)

    barrier = pltpu.get_barrier_semaphore()
    peers = [to_z(j) for j in zs_other] + [to_x(j) for j in xs_other] + [to_y(y2), to_f, to_b, to_p]
    for peer in peers:
        pl.semaphore_signal(barrier, inc=1, device_id=peer, device_id_type=MESH)

    loads = [pltpu.make_async_copy(a, b, in_s.at[i]) for i, (a, b) in enumerate(
        [(k_hbm.at[0], k), (v_hbm.at[0], v), (w_hbm, wx.at[x]), (q_hbm.at[0], q), (g_hbm.at[0], g)])]
    for load in loads:
        load.start()

    loads[0].wait()
    loads[1].wait()

    def kv_head(h, _):
        kvs[h // hx, h % hx] = mm(k[:, cols(h)], v[:, cols(h)], TN).astype(BF16)
        return 0

    lax.fori_loop(0, HEADS, kv_head, 0)
    pl.semaphore_wait(barrier, len(peers))

    for i, j in enumerate(xs_other):
        send(w_hbm, wx.at[x], wx_s.at[i], wx_r.at[x], to_x(j))

    def scan_x_send(n, snd, recv):
        for i, j in enumerate(xs_other):
            send(snd.at[j], recv.at[x], sx_s.at[n, i], sx_r.at[n, x], to_x(j))
        recv[x] = snd[x]

    def scan_z_send(n, recv, out, ring):
        for i, j in enumerate(xs_other):
            arrived(recv.at[j], sx_s.at[n, i], sx_r.at[n, j], to_x(j))
        total = recv[0].astype(F32)
        for j in range(1, nx):
            total = total + recv[j].astype(F32)
        total = total.astype(BF16)
        for i in range(hx):
            out[:, i] = total[i].reshape(nz, hd // nz, hd)
        for i, j in enumerate(zs_other):
            send(out.at[j], ring.at[z], sz_s.at[n, 0, i], sz_r.at[n, 0, z], to_z(j))
        ring[z] = out[z]

    def scan_z_back(n, ring, out, back, reverse):
        for i, j in enumerate(zs_other):
            arrived(ring.at[j], sz_s.at[n, 0, i], sz_r.at[n, 0, j], to_z(j))
        acc = jnp.zeros(ring.shape[1:], F32)
        for zz in (range(nz - 1, -1, -1) if reverse else range(nz)):
            out[zz] = acc.astype(BF16)
            acc = acc + ring[zz].astype(F32)
        for i, j in enumerate(zs_other):
            send(out.at[j], back.at[z], sz_s.at[n, 1, i], sz_r.at[n, 1, z], to_z(j))
        back[z] = out[z]

    def scan_x_back(n, recv, back, out, state, reverse):
        for i, j in enumerate(zs_other):
            arrived(back.at[j], sz_s.at[n, 1, i], sz_r.at[n, 1, j], to_z(j))
        for i in range(hx):
            acc = back[:, i].reshape(hd, hd).astype(F32)
            for j in (range(nx - 1, -1, -1) if reverse else range(nx)):
                out[j, i] = acc.astype(BF16)
                acc = acc + recv[j, i].astype(F32)
        for i, j in enumerate(xs_other):
            send(out.at[j], state.at[x], sb_s.at[n, i], sb_r.at[n, x], to_x(j))
        state[x] = out[x]

    def scan_wait(n, state):
        for i, j in enumerate(xs_other):
            arrived(state.at[j], sb_s.at[n, i], sb_r.at[n, j], to_x(j))

    scan_x_send(0, kvs, ra)

    loads[3].wait()
    causal = (lax.broadcasted_iota(jnp.int32, (tokens, tokens), 0)
              >= lax.broadcasted_iota(jnp.int32, (tokens, tokens), 1))

    def attn_head(h, _):
        a = jnp.where(causal, mm(q[:, cols(h)], k[:, cols(h)], NT), 0.0).astype(BF16)
        attn[h] = a
        outp[:, cols(h)] = mm(a, v[:, cols(h)])
        return 0

    lax.fori_loop(0, 2, attn_head, 0)

    for i, j in enumerate(xs_other):
        arrived(wx.at[j], wx_s.at[i], wx_r.at[j], to_x(j))
    loads[2].wait()
    for j in range(nx):
        asm[j * rows:(j + 1) * rows, :] = wx[j].astype(F32)

    def wblk(yy, zz):
        return wbuf.at[(yy * CORES + c) * nz + zz]

    wbuf[me_dp * nz + z] = asm[...].astype(BF16)

    def w_z(zz, offset, slot):
        send(wblk(y, zz), wblk(y, zz), wz_s.at[slot], wz_r.at[zz], to_z((z + offset + nz) % nz))

    def w_z_arrived(zz):
        arrived(wblk(y, zz), wz_s.at[0], wz_r.at[zz], to_p)

    def w_column(zz):
        send(wblk(y, zz), wblk(y, zz), wy_s.at[0, zz], wy_r.at[0, zz], to_f)
        send(wblk(y, zz), wblk(y, zz), wy_s.at[1, zz], wy_r.at[1, zz], to_b)

    def w_forward(zz):
        arrived(wblk(yb, zz), wy_s.at[2, zz], wy_r.at[0, zz], to_f)
        send(wblk(yb, zz), wblk(yb, zz), wy_s.at[2, zz], wy_r.at[2, zz], to_f)

    def w_group(yy, cc):
        return wbuf.at[pl.ds((yy * CORES + cc) * nz, nz)]

    def w_to_core(yy):
        send(w_group(yy, c), w_group(yy, c), wp_s.at[yy], wp_r.at[yy], to_p)

    far = nz == 8
    near = [1, -1, 2, -2] if far else ([1, -1, 2] if nz == 4 else [1])
    for slot, offset in enumerate(near):
        w_z(z, offset, slot)
    w_column(z)

    scan_z_send(0, ra, ts, tr)
    lax.fori_loop(2, 4, attn_head, 0)

    order = [z]
    for offset in near:
        zz = (z - offset + nz) % nz
        w_z_arrived(zz)
        if far and offset == 2:
            w_z(zz, 1, 4)
            w_z(zz, 2, 5)
        if far and offset == -2:
            w_z(zz, -1, 6)
        w_column(zz)
        order.append(zz)
    scan_z_back(0, tr, es, er, False)
    w_forward(z)
    lax.fori_loop(4, 6, attn_head, 0)
    for zz in order[1:]:
        w_forward(zz)
    late = []
    for offset in ([3, -3, 4] if far else []):
        zz = (z - offset + nz) % nz
        w_z_arrived(zz)
        w_column(zz)
        late.append(zz)
    scan_x_back(0, ra, er, po, st, False)
    w_to_core(y)
    lax.fori_loop(6, HEADS, attn_head, 0)
    for zz in late:
        w_forward(zz)
    w_to_core(yb)
    order = order + late
    scan_wait(0, st)

    def norm_head(h, _):
        o = outp[:, cols(h)] + mm(q[:, cols(h)], st[h // hx, h % hx])
        inv = 1.0 / jnp.sqrt(jnp.mean(o * o, axis=-1, keepdims=True) + NORM_EPS)
        normed = o * inv
        inv_ref[h] = inv
        outp[:, cols(h)] = normed
        unit[:, cols(h)] = (normed * gain_ref[pl.ds(h, 1), :]).astype(BF16)
        return 0

    lax.fori_loop(0, HEADS, norm_head, 0)
    loads[4].wait()

    def wgrad(yy, cc):
        h = yy * CORES + cc
        return mm(unit[:, cols(h)], g[...], TN).reshape(nz, hd // nz, g.shape[-1])

    for yy in (y2, yb, yf, y):
        wgp[yy] = wgrad(yy, 1 - c).astype(BF16)
        send(wgp.at[yy], prt.at[yy], rp_s.at[yy], rp_r.at[yy], to_p)

    def chip_sum(yy):
        own = wgrad(yy, c)
        arrived(prt.at[yy], rp_s.at[yy], rp_r.at[yy], to_p)
        return own + prt[yy].astype(F32)

    zorder = [(z + o) % nz for o in z_offsets] + [z]

    ys2[...] = chip_sum(y2).astype(BF16)
    for zz in zorder:
        send(ys2.at[zz], yr2.at[zz], ry_s.at[0, zz], ry_r.at[0, zz], to_f)
    for zz in order:
        arrived(wblk(yf, zz), wy_s.at[1, zz], wy_r.at[1, zz], to_b)
    w_to_core(yf)
    ysb[...] = chip_sum(yb).astype(BF16)
    for zz in zorder:
        send(ysb.at[zz], yrs.at[zz], ry_s.at[1, zz], ry_r.at[1, zz], to_b)
    for zz in order:
        arrived(wblk(y2, zz), wy_s.at[2, zz], wy_r.at[2, zz], to_f)
    w_to_core(y2)
    fsum[...] = chip_sum(yf)
    for yy in (y, yb, yf, y2):
        arrived(w_group(yy, 1 - c), wp_s.at[yy], wp_r.at[yy], to_p)

    def grad_pair(p, _):
        w2 = wbuf[pl.ds(p * 2 * nz, 2 * nz)].reshape(2 * hd, wbuf.shape[-1])
        ug2 = mm(g[...], w2, NT)
        for i in range(2):
            h = p * 2 + i
            ug = ug2[:, i * hd:(i + 1) * hd]
            normed = outp[:, cols(h)]
            gx[x, pl.ds(h, 1), :] = jnp.sum(ug * normed, axis=0, keepdims=True)
            scaled = ug * gain_ref[pl.ds(h, 1), :]
            m = jnp.mean(scaled * normed, axis=-1, keepdims=True)
            a = ((scaled - normed * m) * inv_ref[h]).astype(BF16)
            ag[:, cols(h)] = a
            qgs[h // hx, h % hx] = mm(q[:, cols(h)], a, TN).astype(BF16)
        return 0

    lax.fori_loop(0, HEADS // 2, grad_pair, 0)

    scan_x_send(1, qgs, rra)
    for i, j in enumerate(xs_other):
        send(gx.at[x], gx.at[x], gx_s.at[i], gx_r.at[x], to_x(j))

    def y_forward(zz):
        arrived(yr2.at[zz], ry_s.at[0, zz], ry_r.at[0, zz], to_f)
        ysf[zz] = (fsum[zz] + yr2[zz].astype(F32)).astype(BF16)
        send(ysf.at[zz], yrc.at[zz], ry_s.at[2, zz], ry_r.at[2, zz], to_f)

    def block(zz):
        arrived(yrc.at[zz], ry_s.at[2, zz], ry_r.at[2, zz], to_f)
        arrived(yrs.at[zz], ry_s.at[1, zz], ry_r.at[1, zz], to_b)
        return wself[zz] + yrc[zz].astype(F32) + yrs[zz].astype(F32)

    def z_send(i):
        j = zorder[i]
        zs[j] = block(j).astype(BF16)
        send(zs.at[j], zr.at[z], rz_s.at[i], rz_r.at[z], to_z(j))

    def grad_head(h, _):
        qh, kh, vh, ah = q[:, cols(h)], k[:, cols(h)], v[:, cols(h)], ag[:, cols(h)]
        sg = jnp.where(causal, mm(ah, vh, NT), 0.0).astype(BF16)
        oq[:, cols(h)] = (mm(sg, kh) + mm(ah, st[h // hx, h % hx], NT)).astype(BF16)
        kpart[:, cols(h)] = mm(sg, qh, TN)
        vpart[:, cols(h)] = mm(attn[h], ah, TN)
        return 0

    for zz in zorder:
        y_forward(zz)
    wself[...] = chip_sum(y)
    lax.fori_loop(0, 4, grad_head, 0)

    scan_z_send(1, rra, rts, rtr)
    for i, j in enumerate(xs_other):
        arrived(gx.at[j], gx_s.at[i], gx_r.at[j], to_x(j))
    gz[z] = jnp.sum(gx[...], axis=0)
    for i, j in enumerate(zs_other):
        send(gz.at[z], gz.at[z], gz_s.at[i], gz_r.at[z], to_z(j))

    lax.fori_loop(4, HEADS, grad_head, 0)
    stores = [pltpu.make_async_copy(oq, qo_hbm.at[0], out_s.at[0])]
    stores[0].start()

    scan_z_back(1, rtr, res, rer, True)
    for i, j in enumerate(zs_other):
        arrived(gz.at[j], gz_s.at[i], gz_r.at[j], to_z(j))
    gy[y] = jnp.sum(gz[...], axis=0)
    for i, j in enumerate((y2, yf, yb)):
        send(gy.at[y], gy.at[y], gy_s.at[i], gy_r.at[y], to_y(j))
    early = (nz - 1) // 2
    for i in range(early):
        z_send(i)
    scan_x_back(1, rra, rer, rpo, rst, True)
    for i, j in enumerate((y2, yf, yb)):
        arrived(gy.at[j], gy_s.at[i], gy_r.at[j], to_y(j))
    gc[c] = jnp.sum(gy[...], axis=0)
    send(gc.at[c], gc.at[c], gc_s.at[0], gc_r.at[0], to_p)
    for i in range(early, nz - 1):
        z_send(i)
    fin = block(z)

    scan_wait(1, rst)

    def last_head(h, _):
        rev = rst[h // hx, h % hx]
        ok[:, cols(h)] = (kpart[:, cols(h)] + mm(v[:, cols(h)], rev, NT)).astype(BF16)
        ov[:, cols(h)] = (vpart[:, cols(h)] + mm(k[:, cols(h)], rev)).astype(BF16)
        return 0

    lax.fori_loop(0, HEADS, last_head, 0)
    for i, (a, b) in enumerate([(ok, ko_hbm), (ov, vo_hbm)]):
        stores.append(pltpu.make_async_copy(a, b.at[0], out_s.at[i + 1]))
        stores[-1].start()

    for i, j in enumerate(zs_other):
        arrived(zr.at[j], rz_s.at[i], rz_r.at[j], to_z(j))
        fin = fin + zr[j].astype(F32)
    for j in range(nx):
        xs[j] = fin[j * rows:(j + 1) * rows, :]
    for i, j in enumerate(xs_other):
        send(xs.at[j], xr.at[x], rx_s.at[i], rx_r.at[x], to_x(j))
    xr[x] = xs[x]
    arrived(gc.at[1 - c], gc_s.at[0], gc_r.at[0], to_p)
    go_ref[...] = (gc[0] + gc[1]) * factor
    for i, j in enumerate(xs_other):
        arrived(xr.at[j], rx_s.at[i], rx_r.at[j], to_x(j))
    wo_ref[...] = jnp.sum(xr[...], axis=0) * factor

    for copy in pending:
        copy.wait_send()
    for store in stores:
        store.wait()


def place(*refs):
    n = (len(refs) - 2) // 3
    src, dst, buf = refs[:n], refs[n:2 * n], refs[2 * n:3 * n]
    in_s, out_s = refs[3 * n:]
    loads = [pltpu.make_async_copy(src[i], buf[i], in_s.at[i]) for i in range(n)]
    stores = [pltpu.make_async_copy(buf[i], dst[i], out_s.at[i]) for i in range(n)]
    for load in loads:
        load.start()
    for load, store in zip(loads, stores):
        load.wait()
        store.start()
    for store in stores:
        store.wait()


def shards(interpret, queries, keys, values, out_grad, out_weight, gain):
    nx = XDIM
    ndp = lax.axis_size("dp")
    nseq = lax.axis_size("seq")
    nz = nseq // nx
    hx = HEADS // nx
    hd = HEAD_DIM
    tok = queries.shape[1]
    d = out_grad.shape[2]
    width = HEADS * hd
    rows = out_weight.shape[0]
    br = rows * nx
    total = tok * ndp * nseq
    factor = 1.0 / float(total) ** 0.5
    vm = pltpu.VMEM
    dma = pltpu.SemaphoreType.DMA
    blocks = vm((nz, br, d), BF16)
    states = vm((nx, hx, hd, hd), BF16)
    ring = vm((nz, hx, hd // nz, hd), BF16)
    flat = vm((tok, width), BF16)
    flat32 = vm((tok, width), F32)
    scan = [states, states, ring, ring, ring, ring, states, states]
    other = max(nx - 1, 1)
    scratch = [
        flat, flat, flat, vm((tok, d), BF16), flat, flat, flat,
        vm((nx, rows, d), BF16), vm((br, d), F32), vm((ndp * nz, br, d), BF16),
        vm((HEADS, tok, tok), BF16), flat32, vm((HEADS, tok, 1), F32), flat, flat, flat32, flat32,
        *scan, *scan,
        vm((YDIM, nz, br, d), BF16), vm((YDIM, nz, br, d), BF16),
        blocks, blocks, blocks, blocks, blocks, blocks, vm((nz, br, d), F32), vm((nz, br, d), F32),
        blocks, blocks, vm((nx, rows, d), F32), vm((nx, rows, d), F32),
        vm((nx, HEADS, hd), F32), vm((nz, HEADS, hd), F32), vm((YDIM, HEADS, hd), F32), vm((CORES, HEADS, hd), F32),
        dma((5,)), dma((3,)), dma((other,)), dma((nx,)), dma((7,)), dma((nz,)),
        dma((3, nz)), dma((3, nz)), dma((YDIM,)), dma((YDIM,)),
        dma((2, other)), dma((2, nx)), dma((2, 2, nz)), dma((2, 2, nz)), dma((2, other)), dma((2, nx)),
        dma((YDIM,)), dma((YDIM,)), dma((3, nz)), dma((3, nz)), dma((nz,)), dma((nz,)),
        dma((other,)), dma((nx,)),
        dma((other,)), dma((nx,)), dma((nz,)), dma((nz,)), dma((3,)), dma((YDIM,)), dma((1,)), dma((1,)),
    ]
    any_spec = pl.BlockSpec(memory_space=pl.ANY)
    vspec = pl.BlockSpec(memory_space=pltpu.VMEM)
    grad = jax.ShapeDtypeStruct((1, tok, width), BF16)
    flops = 2 * tok * width * (2 * d + 6 * tok + 7 * hd)
    shapes = (grad, grad, grad,
              jax.ShapeDtypeStruct((rows, d), F32), jax.ShapeDtypeStruct((HEADS, hd), F32))
    parts = pl.pallas_call(
        functools.partial(kernel, nz, factor),
        out_shape=shapes,
        in_specs=[any_spec] * 5 + [vspec],
        out_specs=(any_spec, any_spec, any_spec, vspec, vspec),
        scratch_shapes=scratch,
        compiler_params=pltpu.CompilerParams(
            collective_id=0, has_side_effects=True, vmem_limit_bytes=62 * 1024 * 1024),
        cost_estimate=pl.CostEstimate(flops=flops, bytes_accessed=16 * 1024 * 1024, transcendentals=0),
        interpret=interpret,
    )(queries, keys, values, out_grad, out_weight, gain.reshape(HEADS, hd))
    qg, kg, vg, wg, gg = pl.pallas_call(
        place,
        out_shape=shapes,
        in_specs=[any_spec] * 5,
        out_specs=(any_spec,) * 5,
        scratch_shapes=[vm(s.shape, s.dtype) for s in shapes] + [dma((5,)), dma((5,))],
        compiler_params=pltpu.CompilerParams(vmem_limit_bytes=62 * 1024 * 1024),
        interpret=interpret,
    )(*parts)
    return qg, kg, vg, wg, gg.reshape(width)


def solution(mesh, interpret=False):
    tokens = P("dp", "seq", None)
    placed = (tokens, tokens, tokens, tokens, P(("dp", "seq"), None), P())
    return jax.shard_map(
        functools.partial(shards, interpret),
        mesh=mesh,
        in_specs=placed,
        out_specs=(tokens, tokens, tokens, P(("dp", "seq"), None), P()),
        check_vma=False,
    )
```

time: 97.4 us -> 83.9 us (0.86)
  Pallas kernels: 90.5 us -> 83.1 us
  local copies, waits for them, and re-layouts: 5.57 us -> 0 us
    pallas_call x1 -> x2, Pallas kernels: 90.5 us -> 83.1 us  [the longest x1 80.2 us: shards(): pl.pallas_call(functools.partial(kernel, nz, factor), out_shape=shapes, i...]
    unnamed x13 -> x0, local copies, waits for them, and re-layouts: 5.57 us -> none
where the time goes in v2:
time: 83.9 us; the launch traced here: 83.8 us
  Pallas kernels  83.1 us (99%)
    pallas_call x1, Pallas kernels, shards(): pl.pallas_call(functools.partial(kernel, nz, factor), out_shape=shapes, i...  80.2 us
    pallas_call x1, Pallas kernels, shards(): pl.pallas_call(place, out_shape=shapes, in_specs=[any_spec] * 5, out_spec...  2.98 us

profile of v2, /device:TPU:2, one launch (start us, length us, event | category | flops | bytes accessed | tf_op | source)
XLA Modules:
  0.0 83.8 jit_solution(14858615380321135764)
XLA Ops:
  0.6 80.2 %shard_map.101 = (bf16[1,512,1024]{2,1,0:T(8,128)(2,1)}, bf16[1,512,1024]{2,1,0:T(8,128)(2,1)}, bf16[1,512,1024]{2,1,0:T(8,128)(2,1)}, f32[4,2048]{1,0:T(4,128)}, f32[8,128]{1,0:T(8,128)}) custom-call(bf16[1,512,1024]{2,1,0:T(8,128)(2,1)} %q_hbm.1, bf16[1,512,1024]{2,1,0:T(8,128)(2,1)} %k_hbm.1, bf16[1,512,1024]{2,1,0:T(8,128)(2,1)} %v_hbm.1, ...), custom_call_target="tpu_custom_call" | custom-call | flops 8455716864 | bytes 16777216 | tf_op jit(solution)/shard_map/pallas_call | solution.py:451
  80.8 3.0 %shard_map.102 = (bf16[1,512,1024]{2,1,0:T(8,128)(2,1)}, bf16[1,512,1024]{2,1,0:T(8,128)(2,1)}, bf16[1,512,1024]{2,1,0:T(8,128)(2,1)}, f32[4,2048]{1,0:T(4,128)}, f32[8,128]{1,0:T(8,128)}) custom-call(bf16[1,512,1024]{2,1,0:T(8,128)(2,1)} %get-tuple-element.15.refs_0_, bf16[1,512,1024]{2,1,0:T(8,128)(2,1)} %get-tuple-element.16.refs_1_, ...), custom_call_target="tpu_custom_call" | custom-call | tf_op jit(solution)/shard_map/pallas_call | solution.py:462

commit v3 on v2

--- a/solution.py
+++ b/solution.py
@@ -26,12 +26,12 @@
 
 
 def kernel(nz, factor, q_hbm, k_hbm, v_hbm, g_hbm, w_hbm, gain_ref,
-           qo_hbm, ko_hbm, vo_hbm, wo_ref, go_ref,
-           q, k, v, g, oq, ok, ov, wx, asm, wbuf, attn, outp, inv_ref, unit, ag, kpart, vpart,
+           oq, ok, ov, wo_ref, go_ref,
+           q, k, v, g, wx, asm, wbuf, attn, outp, inv_ref, unit, ag, kpart, vpart,
            kvs, ra, ts, tr, es, er, po, st, qgs, rra, rts, rtr, res, rer, rpo, rst,
-           wgp, prt, ys2, yr2, ysf, yrc, ysb, yrs, fsum, wself, zs, zr, xs, xr, gx, gz, gy, gc,
-           in_s, out_s, wx_s, wx_r, wz_s, wz_r, wy_s, wy_r, wp_s, wp_r,
-           sx_s, sx_r, sz_s, sz_r, sb_s, sb_r, rp_s, rp_r, ry_s, ry_r, rz_s, rz_r, rx_s, rx_r,
+           wgp, prt, ysend, yrecv, ysum, ysf, yrc, zs, zr, zf, xs, xr, gx, gz, gy, gc,
+           in_s, wx_s, wx_r, wz_s, wz_r, wy_s, wy_r, wp_s, wp_r,
+           sx_s, sx_r, sz_s, sz_r, sb_s, sb_r, rp_s, rp_r, ry_s, ry_r, rz_s, rz_r, rf_r, rx_s, rx_r,
            gx_s, gx_r, gz_s, gz_r, gy_s, gy_r, gc_s, gc_r):
     nx = XDIM
     hx = HEADS // nx
@@ -62,21 +62,28 @@
     to_b = to_y(yb)
     to_p = (y * CORES + 1 - c, me_seq)
 
-    xs_other = [(x + i) % nx for i in ((2, 1, 3) if nx == 4 else range(1, nx))]
+    x_offsets = [2, 1, 3] if nx == 4 else list(range(1, nx))
+    xs_other = [(x + i) % nx for i in x_offsets]
     z_offsets = sorted(range(1, nz), key=lambda o: -min(o, nz - o))
     zs_other = [(z + o) % nz for o in z_offsets]
-
-    pending = []
 
     def send(src, dst, ss, rs, dev):
         copy = pltpu.make_async_remote_copy(
             src_ref=src, dst_ref=dst, send_sem=ss, recv_sem=rs, device_id=dev, device_id_type=MESH)
         copy.start()
-        pending.append(copy)
 
     def arrived(dst, ss, rs, dev):
         pltpu.make_async_remote_copy(
             src_ref=dst, dst_ref=dst, send_sem=ss, recv_sem=rs, device_id=dev, device_id_type=MESH).wait_recv()
+
+    def heads_loop(body, steps):
+        def one(h, _):
+            for at, run in steps:
+                pl.when(h == at)(run)
+            body(h, 0)
+            return 0
+
+        lax.fori_loop(0, HEADS, one, 0)
 
     def cols(h):
         return pl.ds(pl.multiple_of(h * hd, hd), hd)
@@ -161,18 +168,8 @@
         outp[:, cols(h)] = mm(a, v[:, cols(h)])
         return 0
 
-    lax.fori_loop(0, 2, attn_head, 0)
-
-    for i, j in enumerate(xs_other):
-        arrived(wx.at[j], wx_s.at[i], wx_r.at[j], to_x(j))
-    loads[2].wait()
-    for j in range(nx):
-        asm[j * rows:(j + 1) * rows, :] = wx[j].astype(F32)
-
     def wblk(yy, zz):
         return wbuf.at[(yy * CORES + c) * nz + zz]
-
-    wbuf[me_dp * nz + z] = asm[...].astype(BF16)
 
     def w_z(zz, offset, slot):
         send(wblk(y, zz), wblk(y, zz), wz_s.at[slot], wz_r.at[zz], to_z((z + offset + nz) % nz))
@@ -196,40 +193,50 @@
 
     far = nz == 8
     near = [1, -1, 2, -2] if far else ([1, -1, 2] if nz == 4 else [1])
-    for slot, offset in enumerate(near):
-        w_z(z, offset, slot)
-    w_column(z)
-
-    scan_z_send(0, ra, ts, tr)
-    lax.fori_loop(2, 4, attn_head, 0)
-
-    order = [z]
-    for offset in near:
-        zz = (z - offset + nz) % nz
-        w_z_arrived(zz)
-        if far and offset == 2:
-            w_z(zz, 1, 4)
-            w_z(zz, 2, 5)
-        if far and offset == -2:
-            w_z(zz, -1, 6)
-        w_column(zz)
-        order.append(zz)
-    scan_z_back(0, tr, es, er, False)
-    w_forward(z)
-    lax.fori_loop(4, 6, attn_head, 0)
-    for zz in order[1:]:
-        w_forward(zz)
-    late = []
-    for offset in ([3, -3, 4] if far else []):
-        zz = (z - offset + nz) % nz
-        w_z_arrived(zz)
-        w_column(zz)
-        late.append(zz)
+    order = [z] + [(z - o + nz) % nz for o in near]
+    late = [(z - o + nz) % nz for o in ([3, -3, 4] if far else [])]
+
+    def w_rows():
+        for i, j in enumerate(xs_other):
+            arrived(wx.at[j], wx_s.at[i], wx_r.at[j], to_x(j))
+        loads[2].wait()
+        for j in range(nx):
+            asm[j * rows:(j + 1) * rows, :] = wx[j].astype(F32)
+        wbuf[me_dp * nz + z] = asm[...].astype(BF16)
+        for slot, offset in enumerate(near):
+            w_z(z, offset, slot)
+        w_column(z)
+
+    def w_near():
+        for offset, zz in zip(near, order[1:]):
+            w_z_arrived(zz)
+            if far and offset == 2:
+                w_z(zz, 1, 4)
+            if far and offset == -2:
+                w_z(zz, -1, 6)
+                w_z((z - 2 * step + nz) % nz, 2 * step, 5)
+            w_column(zz)
+
+    def w_far():
+        for zz in late:
+            w_z_arrived(zz)
+            w_column(zz)
+
+    def w_forwards(some):
+        for zz in some:
+            w_forward(zz)
+
+    heads_loop(attn_head, [
+        (2, w_rows),
+        (3, lambda: scan_z_send(0, ra, ts, tr)),
+        (4, w_near),
+        (6, lambda: scan_z_back(0, tr, es, er, False)),
+        (6, lambda: w_forwards(order)),
+        (7, w_far),
+    ])
     scan_x_back(0, ra, er, po, st, False)
     w_to_core(y)
-    lax.fori_loop(6, HEADS, attn_head, 0)
-    for zz in late:
-        w_forward(zz)
+    w_forwards(late)
     w_to_core(yb)
     order = order + late
     scan_wait(0, st)
@@ -243,37 +250,73 @@
         unit[:, cols(h)] = (normed * gain_ref[pl.ds(h, 1), :]).astype(BF16)
         return 0
 
-    lax.fori_loop(0, HEADS, norm_head, 0)
     loads[4].wait()
 
     def wgrad(yy, cc):
         h = yy * CORES + cc
+        norm_head(h, 0)
         return mm(unit[:, cols(h)], g[...], TN).reshape(nz, hd // nz, g.shape[-1])
 
-    for yy in (y2, yb, yf, y):
+    def ring_y(i):
+        return (y + 2 + step * i + 2 * YDIM) % YDIM
+
+    def to_partner(i, _):
+        yy = ring_y(i)
         wgp[yy] = wgrad(yy, 1 - c).astype(BF16)
         send(wgp.at[yy], prt.at[yy], rp_s.at[yy], rp_r.at[yy], to_p)
+        return 0
+
+    lax.fori_loop(0, YDIM, to_partner, 0)
 
     def chip_sum(yy):
         own = wgrad(yy, c)
         arrived(prt.at[yy], rp_s.at[yy], rp_r.at[yy], to_p)
         return own + prt[yy].astype(F32)
 
-    zorder = [(z + o) % nz for o in z_offsets] + [z]
-
-    ys2[...] = chip_sum(y2).astype(BF16)
-    for zz in zorder:
-        send(ys2.at[zz], yr2.at[zz], ry_s.at[0, zz], ry_r.at[0, zz], to_f)
-    for zz in order:
-        arrived(wblk(yf, zz), wy_s.at[1, zz], wy_r.at[1, zz], to_b)
-    w_to_core(yf)
-    ysb[...] = chip_sum(yb).astype(BF16)
-    for zz in zorder:
-        send(ysb.at[zz], yrs.at[zz], ry_s.at[1, zz], ry_r.at[1, zz], to_b)
-    for zz in order:
-        arrived(wblk(y2, zz), wy_s.at[2, zz], wy_r.at[2, zz], to_f)
-    w_to_core(y2)
-    fsum[...] = chip_sum(yf)
+    def y_forward(zz):
+        arrived(yrecv.at[0, zz], ry_s.at[0, zz], ry_r.at[0, zz], to_f)
+        ysf[zz] = (ysum[1, zz] + yrecv[0, zz].astype(F32)).astype(BF16)
+        send(ysf.at[zz], yrc.at[zz], ry_s.at[2, zz], ry_r.at[2, zz], to_f)
+
+    if far:
+        z_targets = [4, 3, -3, 2 * step, -2 * step, 1, -1]
+        zorder = [(z + o + nz) % nz for o in z_targets] + [z]
+        z_first = [(2 * step, 1), (1, 0), (-1, 2)]
+    else:
+        zorder = [(z + o) % nz for o in z_offsets] + [z]
+
+    def to_ring(i, _):
+        total = chip_sum(ring_y(i))
+
+        @pl.when(i < 2)
+        def _():
+            ysend[i] = total.astype(BF16)
+            for zz in zorder:
+                send(ysend.at[i, zz], yrecv.at[i, zz], ry_s.at[i, zz], ry_r.at[i, zz],
+                     to_y((y + step * (1 - 2 * i) + YDIM) % YDIM))
+
+        @pl.when(i >= 2)
+        def _():
+            ysum[i - 2] = total
+
+        @pl.when(i == 0)
+        def _():
+            for zz in order:
+                arrived(wblk(yf, zz), wy_s.at[1, zz], wy_r.at[1, zz], to_b)
+            w_to_core(yf)
+
+        @pl.when(i == 2)
+        def _():
+            for zz in order:
+                arrived(wblk(y2, zz), wy_s.at[2, zz], wy_r.at[2, zz], to_f)
+            w_to_core(y2)
+
+        return 0
+
+    lax.fori_loop(0, YDIM, to_ring, 0)
+    cut = nz // 4
+    for zz in zorder[:2 * cut]:
+        y_forward(zz)
     for yy in (y, yb, yf, y2):
         arrived(w_group(yy, 1 - c), wp_s.at[yy], wp_r.at[yy], to_p)
 
@@ -292,112 +335,155 @@
             qgs[h // hx, h % hx] = mm(q[:, cols(h)], a, TN).astype(BF16)
         return 0
 
-    lax.fori_loop(0, HEADS // 2, grad_pair, 0)
-
-    scan_x_send(1, qgs, rra)
+    todo = zorder[2 * cut:]
+    def some_pairs(i, _):
+        p = (x + 1 + i) % nx
+        for j in range(hx // 2):
+            grad_pair(p * (hx // 2) + j, 0)
+
+        @pl.when(i < nx - 1)
+        def _():
+            send(qgs.at[p], rra.at[x], sx_s.at[1, i], sx_r.at[1, x], to_x(p))
+
+        for at in range(nx):
+            @pl.when(i == at)
+            def _():
+                for zz in todo[len(todo) * at // nx:len(todo) * (at + 1) // nx]:
+                    y_forward(zz)
+
+        return 0
+
+    lax.fori_loop(0, nx, some_pairs, 0)
+    rra[x] = qgs[x]
+
     for i, j in enumerate(xs_other):
         send(gx.at[x], gx.at[x], gx_s.at[i], gx_r.at[x], to_x(j))
 
-    def y_forward(zz):
-        arrived(yr2.at[zz], ry_s.at[0, zz], ry_r.at[0, zz], to_f)
-        ysf[zz] = (fsum[zz] + yr2[zz].astype(F32)).astype(BF16)
-        send(ysf.at[zz], yrc.at[zz], ry_s.at[2, zz], ry_r.at[2, zz], to_f)
-
     def block(zz):
         arrived(yrc.at[zz], ry_s.at[2, zz], ry_r.at[2, zz], to_f)
-        arrived(yrs.at[zz], ry_s.at[1, zz], ry_r.at[1, zz], to_b)
-        return wself[zz] + yrc[zz].astype(F32) + yrs[zz].astype(F32)
+        arrived(yrecv.at[1, zz], ry_s.at[1, zz], ry_r.at[1, zz], to_b)
+        return ysum[0, zz] + yrc[zz].astype(F32) + yrecv[1, zz].astype(F32)
+
+    def z_share(n):
+        arrived(zf.at[n], rz_s.at[0], rf_r.at[n], to_p)
+        return zf[n].astype(F32)
 
     def z_send(i):
         j = zorder[i]
-        zs[j] = block(j).astype(BF16)
+        total = block(j)
+        if far and i < 3:
+            offset, n = z_first[i]
+            zs[j] = total.astype(BF16)
+            send(zs.at[j], zf.at[n], rz_s.at[i], rf_r.at[n], to_z((z + offset + nz) % nz))
+            return
+        if far and i == 3:
+            total = total + z_share(1) + z_share(1 - step)
+        if far and i == 4:
+            total = total + z_share(1 + step)
+        zs[j] = total.astype(BF16)
         send(zs.at[j], zr.at[z], rz_s.at[i], rz_r.at[z], to_z(j))
 
     def grad_head(h, _):
         qh, kh, vh, ah = q[:, cols(h)], k[:, cols(h)], v[:, cols(h)], ag[:, cols(h)]
         sg = jnp.where(causal, mm(ah, vh, NT), 0.0).astype(BF16)
-        oq[:, cols(h)] = (mm(sg, kh) + mm(ah, st[h // hx, h % hx], NT)).astype(BF16)
+        oq[0, :, cols(h)] = (mm(sg, kh) + mm(ah, st[h // hx, h % hx], NT)).astype(BF16)
         kpart[:, cols(h)] = mm(sg, qh, TN)
         vpart[:, cols(h)] = mm(attn[h], ah, TN)
         return 0
 
-    for zz in zorder:
-        y_forward(zz)
-    wself[...] = chip_sum(y)
-    lax.fori_loop(0, 4, grad_head, 0)
-
-    scan_z_send(1, rra, rts, rtr)
-    for i, j in enumerate(xs_other):
-        arrived(gx.at[j], gx_s.at[i], gx_r.at[j], to_x(j))
-    gz[z] = jnp.sum(gx[...], axis=0)
-    for i, j in enumerate(zs_other):
-        send(gz.at[z], gz.at[z], gz_s.at[i], gz_r.at[z], to_z(j))
-
-    lax.fori_loop(4, HEADS, grad_head, 0)
-    stores = [pltpu.make_async_copy(oq, qo_hbm.at[0], out_s.at[0])]
-    stores[0].start()
-
-    scan_z_back(1, rtr, res, rer, True)
-    for i, j in enumerate(zs_other):
-        arrived(gz.at[j], gz_s.at[i], gz_r.at[j], to_z(j))
-    gy[y] = jnp.sum(gz[...], axis=0)
-    for i, j in enumerate((y2, yf, yb)):
-        send(gy.at[y], gy.at[y], gy_s.at[i], gy_r.at[y], to_y(j))
-    early = (nz - 1) // 2
-    for i in range(early):
-        z_send(i)
+    def z_sends(first, upto):
+        for i in range(first, min(upto, nz - 1)):
+            z_send(i)
+
+    def gain_z():
+        for i, j in enumerate(xs_other):
+            arrived(gx.at[j], gx_s.at[i], gx_r.at[j], to_x(j))
+        gz[z] = jnp.sum(gx[...], axis=0)
+        for i, j in enumerate(zs_other):
+            send(gz.at[z], gz.at[z], gz_s.at[i], gz_r.at[z], to_z(j))
+
+    def gain_y():
+        for i, j in enumerate(zs_other):
+            arrived(gz.at[j], gz_s.at[i], gz_r.at[j], to_z(j))
+        gy[y] = jnp.sum(gz[...], axis=0)
+        for i, j in enumerate((y2, yf, yb)):
+            send(gy.at[y], gy.at[y], gy_s.at[i], gy_r.at[y], to_y(j))
+
+    heads_loop(grad_head, [
+        (2, lambda: z_sends(0, 1)),
+        (4, lambda: scan_z_send(1, rra, rts, rtr)),
+        (4, gain_z),
+        (4, lambda: z_sends(1, 3)),
+        (6, lambda: z_sends(3, 4)),
+        (7, lambda: scan_z_back(1, rtr, res, rer, True)),
+        (7, gain_y),
+        (7, lambda: z_sends(4, 6)),
+    ])
+    z_sends(6, nz)
     scan_x_back(1, rra, rer, rpo, rst, True)
     for i, j in enumerate((y2, yf, yb)):
         arrived(gy.at[j], gy_s.at[i], gy_r.at[j], to_y(j))
     gc[c] = jnp.sum(gy[...], axis=0)
     send(gc.at[c], gc.at[c], gc_s.at[0], gc_r.at[0], to_p)
-    for i in range(early, nz - 1):
-        z_send(i)
     fin = block(z)
 
-    scan_wait(1, rst)
-
-    def last_head(h, _):
-        rev = rst[h // hx, h % hx]
-        ok[:, cols(h)] = (kpart[:, cols(h)] + mm(v[:, cols(h)], rev, NT)).astype(BF16)
-        ov[:, cols(h)] = (vpart[:, cols(h)] + mm(k[:, cols(h)], rev)).astype(BF16)
-        return 0
-
-    lax.fori_loop(0, HEADS, last_head, 0)
-    for i, (a, b) in enumerate([(ok, ko_hbm), (ov, vo_hbm)]):
-        stores.append(pltpu.make_async_copy(a, b.at[0], out_s.at[i + 1]))
-        stores[-1].start()
-
-    for i, j in enumerate(zs_other):
-        arrived(zr.at[j], rz_s.at[i], rz_r.at[j], to_z(j))
+    for j in ([(z + o + nz) % nz for o in near] if far else zs_other):
+        arrived(zr.at[j], rz_s.at[0], rz_r.at[j], to_z(j))
         fin = fin + zr[j].astype(F32)
     for j in range(nx):
         xs[j] = fin[j * rows:(j + 1) * rows, :]
     for i, j in enumerate(xs_other):
         send(xs.at[j], xr.at[x], rx_s.at[i], rx_r.at[x], to_x(j))
     xr[x] = xs[x]
+
+    scan_wait(1, rst)
+
+    def last_head(h, _):
+        rev = rst[h // hx, h % hx]
+        ok[0, :, cols(h)] = (kpart[:, cols(h)] + mm(v[:, cols(h)], rev, NT)).astype(BF16)
+        ov[0, :, cols(h)] = (vpart[:, cols(h)] + mm(k[:, cols(h)], rev)).astype(BF16)
+        return 0
+
+    lax.fori_loop(0, HEADS, last_head, 0)
+
     arrived(gc.at[1 - c], gc_s.at[0], gc_r.at[0], to_p)
     go_ref[...] = (gc[0] + gc[1]) * factor
     for i, j in enumerate(xs_other):
         arrived(xr.at[j], rx_s.at[i], rx_r.at[j], to_x(j))
     wo_ref[...] = jnp.sum(xr[...], axis=0) * factor
 
-    for copy in pending:
-        copy.wait_send()
+    def left(src, ss):
+        pltpu.make_async_remote_copy(
+            src_ref=src, dst_ref=src, send_sem=ss, recv_sem=ss, device_id=to_p, device_id_type=MESH).wait_send()
+
+    for i in range(nx - 1):
+        for src, ss in ((w_hbm, wx_s.at[i]), (kvs.at[0], sx_s.at[0, i]), (qgs.at[0], sx_s.at[1, i]),
+                        (po.at[0], sb_s.at[0, i]), (rpo.at[0], sb_s.at[1, i]),
+                        (gx.at[0], gx_s.at[i]), (xs.at[0], rx_s.at[i])):
+            left(src, ss)
+    for i in range(nz - 1):
+        for n in range(2):
+            left(ts.at[0], sz_s.at[n, 0, i])
+            left(ts.at[0], sz_s.at[n, 1, i])
+        left(gz.at[0], gz_s.at[i])
+        left(zs.at[0], rz_s.at[i])
+    for i in range(len(near) + len(late)):
+        left(wbuf.at[0], wz_s.at[i])
+    for i in range(3):
+        for zz in range(nz):
+            left(wbuf.at[0], wy_s.at[i, zz])
+            left(ysf.at[0], ry_s.at[i, zz])
+        left(gy.at[0], gy_s.at[i])
+    for yy in range(YDIM):
+        left(w_group(0, 0), wp_s.at[yy])
+        left(wgp.at[0], rp_s.at[yy])
+    left(gc.at[0], gc_s.at[0])
+
+
+def place(*refs):
+    n = len(refs) // 2
+    stores = [pltpu.make_async_copy(refs[i], refs[n + i], refs[2 * n].at[i]) for i in range(n)]
     for store in stores:
-        store.wait()
-
-
-def place(*refs):
-    n = (len(refs) - 2) // 3
-    src, dst, buf = refs[:n], refs[n:2 * n], refs[2 * n:3 * n]
-    in_s, out_s = refs[3 * n:]
-    loads = [pltpu.make_async_copy(src[i], buf[i], in_s.at[i]) for i in range(n)]
-    stores = [pltpu.make_async_copy(buf[i], dst[i], out_s.at[i]) for i in range(n)]
-    for load in loads:
-        load.start()
-    for load, store in zip(loads, stores):
-        load.wait()
         store.start()
     for store in stores:
         store.wait()
@@ -427,18 +513,18 @@
     scan = [states, states, ring, ring, ring, ring, states, states]
     other = max(nx - 1, 1)
     scratch = [
-        flat, flat, flat, vm((tok, d), BF16), flat, flat, flat,
+        flat, flat, flat, vm((tok, d), BF16),
         vm((nx, rows, d), BF16), vm((br, d), F32), vm((ndp * nz, br, d), BF16),
         vm((HEADS, tok, tok), BF16), flat32, vm((HEADS, tok, 1), F32), flat, flat, flat32, flat32,
         *scan, *scan,
         vm((YDIM, nz, br, d), BF16), vm((YDIM, nz, br, d), BF16),
-        blocks, blocks, blocks, blocks, blocks, blocks, vm((nz, br, d), F32), vm((nz, br, d), F32),
-        blocks, blocks, vm((nx, rows, d), F32), vm((nx, rows, d), F32),
+        vm((2, nz, br, d), BF16), vm((2, nz, br, d), BF16), vm((2, nz, br, d), F32), blocks, blocks,
+        blocks, blocks, vm((3, br, d), BF16), vm((nx, rows, d), F32), vm((nx, rows, d), F32),
         vm((nx, HEADS, hd), F32), vm((nz, HEADS, hd), F32), vm((YDIM, HEADS, hd), F32), vm((CORES, HEADS, hd), F32),
-        dma((5,)), dma((3,)), dma((other,)), dma((nx,)), dma((7,)), dma((nz,)),
+        dma((5,)), dma((other,)), dma((nx,)), dma((7,)), dma((nz,)),
         dma((3, nz)), dma((3, nz)), dma((YDIM,)), dma((YDIM,)),
         dma((2, other)), dma((2, nx)), dma((2, 2, nz)), dma((2, 2, nz)), dma((2, other)), dma((2, nx)),
-        dma((YDIM,)), dma((YDIM,)), dma((3, nz)), dma((3, nz)), dma((nz,)), dma((nz,)),
+        dma((YDIM,)), dma((YDIM,)), dma((3, nz)), dma((3, nz)), dma((nz,)), dma((nz,)), dma((3,)),
         dma((other,)), dma((nx,)),
         dma((other,)), dma((nx,)), dma((nz,)), dma((nz,)), dma((3,)), dma((YDIM,)), dma((1,)), dma((1,)),
     ]
@@ -452,20 +538,20 @@
         functools.partial(kernel, nz, factor),
         out_shape=shapes,
         in_specs=[any_spec] * 5 + [vspec],
-        out_specs=(any_spec, any_spec, any_spec, vspec, vspec),
+        out_specs=(vspec,) * 5,
         scratch_shapes=scratch,
         compiler_params=pltpu.CompilerParams(
-            collective_id=0, has_side_effects=True, vmem_limit_bytes=62 * 1024 * 1024),
+            collective_id=0, has_side_effects=True, vmem_limit_bytes=51600 * 1 * 1024),
         cost_estimate=pl.CostEstimate(flops=flops, bytes_accessed=16 * 1024 * 1024, transcendentals=0),
         interpret=interpret,
     )(queries, keys, values, out_grad, out_weight, gain.reshape(HEADS, hd))
     qg, kg, vg, wg, gg = pl.pallas_call(
         place,
         out_shape=shapes,
-        in_specs=[any_spec] * 5,
+        in_specs=[vspec] * 5,
         out_specs=(any_spec,) * 5,
-        scratch_shapes=[vm(s.shape, s.dtype) for s in shapes] + [dma((5,)), dma((5,))],
-        compiler_params=pltpu.CompilerParams(vmem_limit_bytes=62 * 1024 * 1024),
+        scratch_shapes=[dma((5,))],
+        compiler_params=pltpu.CompilerParams(vmem_limit_bytes=8 * 1024 * 1024),
         interpret=interpret,
     )(*parts)
     return qg, kg, vg, wg, gg.reshape(width)

time: 83.9 us -> 79.1 us (0.943)
  Pallas kernels: 83.1 us -> 76.9 us
  local copies, waits for them, and re-layouts: 0 us -> 1.4 us
    pallas_call x1, Pallas kernels: 80.2 us -> 75.2 us  [shards(): pl.pallas_call(functools.partial(kernel, nz, factor), out_shape=shapes, i...]
    unnamed x0 -> x4, local copies, waits for them, and re-layouts: none -> 1.4 us
    pallas_call x1, Pallas kernels: 2.98 us -> 1.71 us  [shards(): pl.pallas_call(place, out_shape=shapes, in_specs=[vspec] * 5, out_specs=(...]
where the time goes in v3:
time: 79.1 us; the launch traced here: 78.9 us
  Pallas kernels  76.9 us (97%)
  local copies, waits for them, and re-layouts  1.4 us (2%)
    pallas_call x1, Pallas kernels, shards(): pl.pallas_call(functools.partial(kernel, nz, factor), out_shape=shapes, i...  75.2 us
    pallas_call x1, Pallas kernels, shards(): pl.pallas_call(place, out_shape=shapes, in_specs=[vspec] * 5, out_specs=(...  1.71 us

profile of v3, /device:TPU:2, one launch (start us, length us, event | category | flops | bytes accessed | tf_op | source)
XLA Modules:
  0.0 78.9 jit_solution(1852624034032677349)
XLA Ops:
  0.6 0.0 copy-start
  0.6 0.7 copy-done
  1.4 0.0 copy-start.1
  1.4 0.7 copy-done.1
  2.0 75.2 %shard_map.101 = (bf16[1,512,1024]{2,1,0:T(8,128)(2,1)S(1)}, bf16[1,512,1024]{2,1,0:T(8,128)(2,1)S(1)}, bf16[1,512,1024]{2,1,0:T(8,128)(2,1)S(1)}, f32[4,2048]{1,0:T(4,128)S(1)}, f32[8,128]{1,0:T(8,128)S(1)}) custom-call(bf16[1,512,1024]{2,1,0:T(8,128)(2,1)} %q_hbm.1, bf16[1,512,1024]{2,1,0:T(8,128)(2,1)} %k_hbm.1, bf16[1,512,1024]{2,1,0:T(8,128)(2,1)} %v_hbm.1, ...), custom_call_target="tpu_custom_call" | custom-call | flops 8455716864 | bytes 16777216 | tf_op jit(solution)/shard_map/pallas_call | solution.py:537
  77.2 1.7 %shard_map.102 = (bf16[1,512,1024]{2,1,0:T(8,128)(2,1)}, bf16[1,512,1024]{2,1,0:T(8,128)(2,1)}, bf16[1,512,1024]{2,1,0:T(8,128)(2,1)}, f32[4,2048]{1,0:T(4,128)}, f32[8,128]{1,0:T(8,128)}) custom-call(bf16[1,512,1024]{2,1,0:T(8,128)(2,1)S(1)} %get-tuple-element.15.refs_0_, bf16[1,512,1024]{2,1,0:T(8,128)(2,1)S(1)} %get-tuple-element.16.refs_1_, ...), custom_call_target="tpu_custom_call" | custom-call | tf_op jit(solution)/shard_map/pallas_call | solution.py:548
Async XLA Ops:
  0.6 0.7 copy-start
  1.4 0.7 copy-start.1

commit v4 on v3

--- a/solution.py
+++ b/solution.py
@@ -231,8 +231,8 @@
         (3, lambda: scan_z_send(0, ra, ts, tr)),
         (4, w_near),
         (6, lambda: scan_z_back(0, tr, es, er, False)),
+        (6, w_far),
         (6, lambda: w_forwards(order)),
-        (7, w_far),
     ])
     scan_x_back(0, ra, er, po, st, False)
     w_to_core(y)

time: 79.1 us -> 79.1 us (level)
  no operation moved by 1% of the time
where the time goes in v4:
time: 79.1 us; the launch traced here: 78.9 us
  Pallas kernels  76.9 us (97%)
  local copies, waits for them, and re-layouts  1.4 us (2%)
    pallas_call x1, Pallas kernels, shards(): pl.pallas_call(functools.partial(kernel, nz, factor), out_shape=shapes, i...  75.1 us
    pallas_call x1, Pallas kernels, shards(): pl.pallas_call(place, out_shape=shapes, in_specs=[vspec] * 5, out_specs=(...  1.71 us

profile of v4, /device:TPU:2, one launch (start us, length us, event | category | flops | bytes accessed | tf_op | source)
XLA Modules:
  0.0 78.9 jit_solution(14666166656938497135)
XLA Ops:
  0.6 0.0 copy-start
  0.6 0.7 copy-done
  1.4 0.0 copy-start.1
  1.4 0.7 copy-done.1
  2.0 75.1 %shard_map.101 = (bf16[1,512,1024]{2,1,0:T(8,128)(2,1)S(1)}, bf16[1,512,1024]{2,1,0:T(8,128)(2,1)S(1)}, bf16[1,512,1024]{2,1,0:T(8,128)(2,1)S(1)}, f32[4,2048]{1,0:T(4,128)S(1)}, f32[8,128]{1,0:T(8,128)S(1)}) custom-call(bf16[1,512,1024]{2,1,0:T(8,128)(2,1)} %q_hbm.1, bf16[1,512,1024]{2,1,0:T(8,128)(2,1)} %k_hbm.1, bf16[1,512,1024]{2,1,0:T(8,128)(2,1)} %v_hbm.1, ...), custom_call_target="tpu_custom_call" | custom-call | flops 8455716864 | bytes 16777216 | tf_op jit(solution)/shard_map/pallas_call | solution.py:537
  77.2 1.7 %shard_map.102 = (bf16[1,512,1024]{2,1,0:T(8,128)(2,1)}, bf16[1,512,1024]{2,1,0:T(8,128)(2,1)}, bf16[1,512,1024]{2,1,0:T(8,128)(2,1)}, f32[4,2048]{1,0:T(4,128)}, f32[8,128]{1,0:T(8,128)}) custom-call(bf16[1,512,1024]{2,1,0:T(8,128)(2,1)S(1)} %get-tuple-element.15.refs_0_, bf16[1,512,1024]{2,1,0:T(8,128)(2,1)S(1)} %get-tuple-element.16.refs_1_, ...), custom_call_target="tpu_custom_call" | custom-call | tf_op jit(solution)/shard_map/pallas_call | solution.py:548
Async XLA Ops:
  0.6 0.7 copy-start
  1.4 0.7 copy-start.1
